TPU v7x, 32 devices: a whole 2x2x4 slice. The times are simulated.
32 devices in a mesh: dp: 4 (over y, x), mp: 8 (over z, core).
Axes of the slice: x: 2, y: 2, z: 4, core: 2. Of those that a mesh axis runs over, the one named last changes fastest.
Arguments:
- train_acts: bfloat16 [512, 4096], P('dp', 'mp'), may hold values from -6 to 6
- train_grads: bfloat16 [512, 7168], P('dp', 'mp'), may hold values from -0.75 to 0.75
- query_acts: bfloat16 [1024, 4096], P('dp', 'mp'), may hold values from -6 to 6
- query_grads: bfloat16 [1024, 7168], P('dp', 'mp'), may hold values from -0.75 to 0.75
- basis_in: bfloat16 [4096, 4096], P('mp'), may hold values from -0.125 to 0.125
- basis_out: bfloat16 [7168, 7168], P('mp'), may hold values from -0.09375 to 0.09375
- eigvals: bfloat16 [4096, 7168], P(None, 'mp'), may hold values from 0.25 to 4
Outputs:
- scores: float32 [16, 8], P(None, 'dp')
- energies: float32 [8], P('dp')
All inputs are finite; a program needn't handle non-finite values.
Results may differ from a plain program's by a relative error of at most 0.0048.
Values may be sent and summed in bfloat16 or wider, within the bound.
No kernel may reach another device: no remote copies, remote signals or barrier semaphores. Data moves between devices by JAX's collectives and lax.ppermute only.
A program may use at most 128 MiB of HBM per device.

v0:
```python
import math
import jax
import jax.numpy as jnp
from jax import lax
from jax.sharding import PartitionSpec as P

D = 4096
H = 7168
SEQ = 64
damping = 0.1


def pair_scores(query_a, query_g, scaled):
    applied = jnp.einsum("it,nij->ntj", query_a, scaled, preferred_element_type=jnp.float32)
    per_token = jnp.sum(applied * jnp.transpose(query_g).astype(jnp.float32)[None], axis=2)
    grouped = jnp.sum(per_token.reshape(per_token.shape[0], -1, SEQ), axis=2)
    return jnp.transpose(grouped)


def on_device(train_acts, train_grads, query_acts, query_grads, basis_in, basis_out, eigvals):
    train_rows = train_acts.shape[0]
    train_seqs = train_rows // SEQ
    acts = jnp.concatenate([train_acts, query_acts], axis=0)
    grads = jnp.concatenate([train_grads, query_grads], axis=0)
    columns = basis_in
    rot_acts = lax.psum(
        jnp.einsum("fc,rf->cr", columns, acts, preferred_element_type=jnp.float32), "mp"
    ).astype(jnp.bfloat16)
    columns = basis_out
    rot_grads = lax.psum_scatter(
        jnp.einsum("fc,rf->cr", columns, grads, preferred_element_type=jnp.float32),
        "mp",
        scatter_dimension=0,
        tiled=True,
    ).astype(jnp.bfloat16)
    train_a = rot_acts[:, :train_rows].reshape(rot_acts.shape[0], train_seqs, SEQ)
    train_g = rot_grads[:, :train_rows].reshape(rot_grads.shape[0], train_seqs, SEQ)
    query_a = rot_acts[:, train_rows:]
    query_g = rot_grads[:, train_rows:]
    train_outer = jnp.einsum("isk,jsk->sij", train_a, train_g, preferred_element_type=jnp.float32)
    shifted = eigvals.astype(jnp.float32) + damping
    scaled = (train_outer / shifted).astype(jnp.bfloat16)
    energy_part = jnp.sum(train_outer * train_outer, axis=(1, 2))
    all_query_a, all_query_g = (
        lax.all_gather(query_a, "dp", axis=1, tiled=True),
        lax.all_gather(query_g, "dp", axis=1, tiled=True),
    )
    partial_value = pair_scores(all_query_a, all_query_g, scaled)
    total_scores, total_energy = lax.psum((partial_value, energy_part), "mp")
    scores = total_scores * (1.0 / math.sqrt(D * H))
    energies = total_energy / (D * H)
    return (scores, energies)


def solution(mesh):
    return jax.shard_map(
        on_device,
        mesh=mesh,
        in_specs=(
            P("dp", "mp"),
            P("dp", "mp"),
            P("dp", "mp"),
            P("dp", "mp"),
            P("mp", None),
            P("mp", None),
            P(None, "mp"),
        ),
        out_specs=(P(None, "dp"), P("dp")),
        check_vma=False,
    )
```

profile of v0, /device:TPU:0, one launch (start us, length us, event | category | flops | bytes accessed | tf_op | source)
XLA Modules:
  0.0 401.3 jit_solution(1922817455804115351)
XLA Ops:
  7.2 0.0 reduce-scatter.2.cloned.1.call-start
  7.2 11.4 %convolution_bitcast_fusion = f32[7168,384]{0,1:T(8,128)} fusion(bf16[896,7168]{1,0:T(8,128)(2,1)} %param.12, bf16[256,896]{1,0:T(8,128)(2,1)} %param.10, bf16[128,896]{1,0:T(8,128)(2,1)} %param.8), kind=kOutput, calls=%fused_computation.4 | convolution fusion | flops 4933877760 | bytes 24543232 | tf_op jit(solution)/shard_map/fc,rf->cr/dot_general | solution.py:31
  18.7 0.0 copy-start.1
  18.7 0.0 reduce-scatter.2.cloned.1.call-update
  18.7 0.0 all-gather.5.cloned.1.call-start
  18.7 0.9 copy-done.1
  19.6 0.0 copy-done.2
  19.6 6.6 %convolution_bitcast_fusion.1 = f32[4096,384]{0,1:T(8,128)} fusion(bf16[512,4096]{1,0:T(8,128)(2,1)} %param.11, bf16[256,512]{1,0:T(8,128)(2,1)S(1)} %copy-done.1, bf16[128,512]{1,0:T(8,128)(2,1)S(1)} %copy-done.2), kind=kOutput, calls=%fused_computation.8 | convolution fusion | flops 1611399168 | bytes 10878976 | tf_op jit(solution)/shard_map/fc,rf->cr/dot_general | solution.py:27
  26.2 109.6 %reduce-scatter.2.cloned.1.call-done = f32[896,384]{0,1:T(8,128)} async-done(((f32[7168,384]{0,1:T(8,128)}), f32[896,384]{0,1:T(8,128)}) %reduce-scatter.2.cloned.1.call-update) | async-done | bytes 1376272 | tf_op jit(solution)/shard_map/reduce_scatter | solution.py:30
  135.8 1.4 convert_element_type.19
  137.3 0.0 copy-start
  137.3 0.8 copy-done
  138.1 0.8 slice.19
  138.9 0.0 all-gather.5.cloned.1.call-update
  138.9 0.0 all-gather.3.cloned.1.call-start
  139.0 127.1 %all-reduce.2 = bf16[4096,384]{0,1:T(8,128)(2,1)S(1)} all-reduce(f32[4096,384]{0,1:T(8,128)} %convolution_bitcast_fusion.1), channel_id=1, replica_groups=mesh['dp'=4,'mp'=8] {'mp'}, use_global_device_ids=true, to_apply=%region_0.0 | all-reduce | flops 1572864 | bytes 9437184 | tf_op jit(solution)/shard_map/psum | solution.py:26
  266.1 1.5 slice.18
  267.5 0.0 all-gather.3.cloned.1.call-update
  267.6 0.1 slice.16
  267.6 0.0 slice-start
  267.7 11.2 %convert_add_fusion = f32[4096,896]{1,0:T(8,128)} fusion(bf16[4096,896]{1,0:T(8,128)(2,1)} %param.13), kind=kLoop, calls=%fused_computation.2 | loop fusion | flops 7340032 | bytes 22020096 | tf_op jit(solution)/shard_map/add | solution.py:41
  278.8 0.0 slice-done
  278.8 12.1 %multiply_reduce_fusion = (f32[2]{0:T(128)S(1)}, f32[2,4096,896]{2,1,0:T(8,128)}) fusion(bf16[4096,2,64]{0,2,1:T(8,128)(2,1)S(1)} %bitcast.22, bf16[896,2,64]{0,2,1:T(8,128)(2,1)S(1)} %bitcast.23), kind=kOutput, calls=%fused_computation | convolution fusion | flops 954204160 | bytes 30638088 | tf_op jit(solution)/shard_map/isk,jsk->sij/dot_general | solution.py:40
  290.9 3.6 convert_bitcast_fusion
  294.5 5.0 %copy.14 = f32[1024,896]{0,1:T(8,128)} copy(f32[1024,896]{1,0:T(8,128)} %convert_bitcast_fusion) | data formatting | bytes 7340032 | tf_op jit(solution)/shard_map/convert_element_type | solution.py:15
  299.5 54.0 %all-gather.3.cloned.1.call-done = bf16[4096,1024]{0,1:T(8,128)(2,1)} async-done(((bf16[4096,256]{0,1:T(8,128)(2,1)}), bf16[4096,1024]{0,1:T(8,128)(2,1)}) %all-gather.3.cloned.1.call-update) | async-done | bytes 8388624 | tf_op jit(solution)/shard_map/all_gather | solution.py:45
  353.5 23.9 %fusion.2 = f32[2,1024]{1,0:T(2,128)S(1)} fusion(f32[1024,896]{0,1:T(8,128)} %copy.14, bf16[4096,1024]{0,1:T(8,128)(2,1)} %all-gather.3.cloned.1.call-done, f32[2,4096,896]{2,1,0:T(8,128)} %get-tuple-element.5, f32[4096,896]{1,0:T(8,128)} %convert_add_fusion), kind=kOutput, calls=%fused_computation.7 | convolution fusion | flops 15050733568 | bytes 56107008 | tf_op jit(solution)/shard_map/it,nij->ntj/dot_general | solution.py:14
  377.4 0.1 reshape.17
  377.5 0.1 reduce_sum.28
  377.6 16.2 %all-reduce = (f32[16,2]{0,1:T(2,128)S(1)}, f32[2]{0:T(128)S(1)}) all-reduce(f32[16,2]{0,1:T(2,128)S(1)} %bitcast.24, f32[2]{0:T(128)S(1)} %get-tuple-element.4), channel_id=1, replica_groups=mesh['dp'=4,'mp'=8] {'mp'}, use_global_device_ids=true, to_apply=%region_4.0 | all-reduce | flops 34 | bytes 272 | tf_op jit(solution)/shard_map/psum | solution.py:49
  393.7 0.6 broadcast_multiply_fusion
  394.3 0.5 broadcast_multiply_fusion.1
  (2 shorter events, 0.0 us)
Async XLA Ops:
  7.2 128.7 %reduce-scatter.2.cloned.1.call-start = ((), (), s32[]{:S(2)}) async-start(), calls=%async_computation.1 | async-start | bytes 12386304 | tf_op jit(solution)/shard_map/reduce_scatter | solution.py:30
  18.7 0.9 copy-start.1
  18.7 1.0 copy-start.2
  18.7 272.2 %all-gather.5.cloned.1.call-start = ((), (), s32[]{:S(2)}) async-start(), calls=%async_computation.3 | async-start | bytes 2293760 | tf_op jit(solution)/shard_map/all_gather | solution.py:46
  137.3 0.9 copy-start
  138.9 214.6 %all-gather.3.cloned.1.call-start = ((), (), s32[]{:S(2)}) async-start(), calls=%async_computation.2 | async-start | bytes 10485760 | tf_op jit(solution)/shard_map/all_gather | solution.py:45
  267.6 11.2 %slice-start = ((bf16[896,384]{0,1:T(8,128)(2,1)}), bf16[896,128]{0,1:T(8,128)(2,1)S(1)}, s32[]{:S(2)}) async-start(bf16[896,384]{0,1:T(8,128)(2,1)} %copy-done), calls=%async_computation.4 | async-start | bytes 458752 | tf_op jit(solution)/shard_map/slice | solution.py:37
Sparse Core Ops, SparseCore 0:
  18.8 117.0 reduce-scatter.1
  139.1 31.4 all-gather.4
  267.7 85.7 all-gather.2
where the time goes:
time: 402 us; the launch traced here: 401 us
  waiting for transfers between devices  164 us (41%)
  blocking collectives  143 us (36%)
  matrix products  53.9 us (13%)
  other arithmetic  17.3 us (4%)
  between operations  13.8 us (3%)
  local copies, waits for them, and re-layouts  9.22 us (2%)
    psum x1, blocking collectives, on_device(): lax.psum(jnp.einsum('fc,rf->cr', columns, acts, preferred_element_type=jn...  127 us
    reduce_scatter x1, waiting for transfers between devices, on_device(): lax.psum_scatter(jnp.einsum('fc,rf->cr', columns, grads, preferred_elemen...  110 us
    all_gather x1, waiting for transfers between devices, on_device(): lax.all_gather(query_a, 'dp', axis=1, tiled=True)  54 us
    dot_general x1, matrix products, pair_scores(): jnp.einsum('it,nij->ntj', query_a, scaled, preferred_element_type=jnp.flo...  23.9 us
    psum x1, blocking collectives, on_device(): total_scores, total_energy = lax.psum((partial_value, energy_part), 'mp')  16.2 us
    dot_general x1, matrix products, on_device(): jnp.einsum('isk,jsk->sij', train_a, train_g, preferred_element_type=jnp.f...  12.1 us
    dot_general x1, matrix products, on_device(): jnp.einsum('fc,rf->cr', columns, grads, preferred_element_type=jnp.float32)  11.4 us
    add x1, other arithmetic, on_device(): shifted = eigvals.astype(jnp.float32) + damping  11.2 us
  transfers between devices with their start and end apart: 3, of which 2 were waited for; matrix products, arithmetic and copies ran while one was open for 10% of the time, Pallas kernels for 0%

commit v1 on v0

--- a/solution.py
+++ b/solution.py
@@ -8,6 +8,19 @@
 H = 7168
 SEQ = 64
 damping = 0.1
+
+
+def ring_gather(x, axis, dim):
+    ways = lax.axis_size(axis)
+    up = [(d, (d + 1) % ways) for d in range(ways)]
+    down = [(d, (d - 1) % ways) for d in range(ways)]
+    earlier, later = ([x], [x])
+    for _ in range(ways // 2):
+        earlier.append(lax.ppermute(earlier[-1], axis, up))
+    for _ in range((ways - 1) // 2):
+        later.append(lax.ppermute(later[-1], axis, down))
+    line = jnp.concatenate([*earlier[::-1], *later[1:]], axis=dim)
+    return jnp.roll(line, (lax.axis_index(axis) - ways // 2) * x.shape[dim], axis=dim)
 
 
 def pair_scores(query_a, query_g, scaled):
@@ -42,7 +55,7 @@
     scaled = (train_outer / shifted).astype(jnp.bfloat16)
     energy_part = jnp.sum(train_outer * train_outer, axis=(1, 2))
     all_query_a, all_query_g = (
-        lax.all_gather(query_a, "dp", axis=1, tiled=True),
+        ring_gather(query_a, "dp", 1),
         lax.all_gather(query_g, "dp", axis=1, tiled=True),
     )
     partial_value = pair_scores(all_query_a, all_query_g, scaled)

time: 402 us -> 494 us (1.23)
  blocking collectives: 143 us -> 245 us
  waiting for transfers between devices: 164 us -> 128 us
  local copies, waits for them, and re-layouts: 9.22 us -> 31.4 us
    ppermute x0 -> x3, waiting for transfers between devices: none -> 113 us  [the longest x2 80.5 us: ring_gather(): earlier.append(lax.ppermute(earlier[-1], axis, up))]
    reduce_scatter x1, waiting for transfers between devices: 110 us -> 0.01 us  [on_device(): lax.psum_scatter(jnp.einsum('fc,rf->cr', columns, grads, preferred_elemen...]
    psum x1, blocking collectives: 127 us -> 229 us  [on_device(): lax.psum(jnp.einsum('fc,rf->cr', columns, acts, preferred_element_type=jn...]
    all_gather x1 -> x0, waiting for transfers between devices: 54 us -> none  [on_device(): lax.all_gather(query_a, 'dp', axis=1, tiled=True)]
    unnamed x6 -> x15, local copies, waits for them, and re-layouts: 1.76 us -> 19.8 us
    all_gather x1, waiting for transfers between devices: 0.01 us -> 15.4 us  [on_device(): lax.all_gather(query_g, 'dp', axis=1, tiled=True)]
  transfers between devices with their start and end apart: 3 -> 5, of which waited for: 2 -> 4; matrix products, arithmetic and copies ran while one was open for 10% -> 11% of each run, Pallas kernels for 0% -> 0%
where the time goes in v1:
time: 494 us; the launch traced here: 493 us
  blocking collectives  245 us (50%)
  waiting for transfers between devices  128 us (26%)
  matrix products  54.3 us (11%)
  local copies, waits for them, and re-layouts  31.4 us (6%)
  other arithmetic  15.7 us (3%)
  between operations  14.1 us (3%)
    psum x1, blocking collectives, on_device(): lax.psum(jnp.einsum('fc,rf->cr', columns, acts, preferred_element_type=jn...  229 us
    ppermute x2, waiting for transfers between devices, ring_gather(): earlier.append(lax.ppermute(earlier[-1], axis, up))  80.5 us
    ppermute x1, waiting for transfers between devices, ring_gather(): later.append(lax.ppermute(later[-1], axis, down))  32.4 us
    dot_general x1, matrix products, pair_scores(): jnp.einsum('it,nij->ntj', query_a, scaled, preferred_element_type=jnp.flo...  24 us
    unnamed x15, local copies, waits for them, and re-layouts  19.8 us
    psum x1, blocking collectives, on_device(): total_scores, total_energy = lax.psum((partial_value, energy_part), 'mp')  16.2 us
    all_gather x1, waiting for transfers between devices, on_device(): lax.all_gather(query_g, 'dp', axis=1, tiled=True)  15.4 us
    dot_general x1, matrix products, on_device(): jnp.einsum('isk,jsk->sij', train_a, train_g, preferred_element_type=jnp.f...  12.3 us
  transfers between devices with their start and end apart: 5, of which 4 were waited for; matrix products, arithmetic and copies ran while one was open for 11% of the time, Pallas kernels for 0%

profile of v1, /device:TPU:0, one launch (start us, length us, event | category | flops | bytes accessed | tf_op | source)
XLA Modules:
  0.0 493.1 jit_solution(12869374078021769901)
XLA Ops:
  7.2 11.5 %convolution_bitcast_fusion = f32[7168,384]{0,1:T(8,128)} fusion(bf16[896,7168]{1,0:T(8,128)(2,1)} %param.12, bf16[256,896]{1,0:T(8,128)(2,1)} %param.10, bf16[128,896]{1,0:T(8,128)(2,1)} %param.8), kind=kOutput, calls=%fused_computation.4 | convolution fusion | flops 4933877760 | bytes 24543232 | tf_op jit(solution)/shard_map/fc,rf->cr/dot_general | solution.py:44
  18.8 6.6 %convolution_bitcast_fusion.1 = f32[4096,384]{0,1:T(8,128)} fusion(bf16[512,4096]{1,0:T(8,128)(2,1)} %param.11, bf16[256,512]{1,0:T(8,128)(2,1)S(1)} %copy-done.2, bf16[128,512]{1,0:T(8,128)(2,1)S(1)} %copy-done.3), kind=kOutput, calls=%fused_computation.9 | convolution fusion | flops 1611399168 | bytes 10878976 | tf_op jit(solution)/shard_map/fc,rf->cr/dot_general | solution.py:40
  25.4 228.6 %all-reduce.2 = bf16[4096,384]{0,1:T(8,128)(2,1)S(1)} all-reduce(f32[4096,384]{0,1:T(8,128)} %convolution_bitcast_fusion.1), channel_id=1, replica_groups=mesh['dp'=4,'mp'=8] {'mp'}, use_global_device_ids=true, to_apply=%region_0.0 | all-reduce | flops 1572864 | bytes 9437184 | tf_op jit(solution)/shard_map/psum | solution.py:39
  254.0 1.6 slice.18
  255.6 1.5 collective-permute-start
  257.0 44.4 %collective-permute-done = bf16[4096,256]{0,1:T(8,128)(2,1)} collective-permute-done((bf16[4096,256]{0,1:T(8,128)(2,1)}, bf16[4096,256]{0,1:T(8,128)(2,1)}, u32[]{:S(2)}, u32[]{:S(2)}) %collective-permute-start) | collective-permute-done | bytes 2097184 | tf_op jit(solution)/shard_map/ppermute | solution.py:19
  301.4 1.4 collective-permute-start.1
  302.8 1.5 collective-permute-start.2
  304.3 9.6 %convert_add_fusion = f32[4096,896]{1,0:T(8,128)} fusion(bf16[4096,896]{1,0:T(8,128)(2,1)} %param.13), kind=kLoop, calls=%fused_computation.2 | loop fusion | flops 7340032 | bytes 22020096 | tf_op jit(solution)/shard_map/add | solution.py:54
  313.9 1.1 slice.16
  315.0 36.1 %collective-permute-done.1 = bf16[4096,256]{0,1:T(8,128)(2,1)} collective-permute-done((bf16[4096,256]{0,1:T(8,128)(2,1)}, bf16[4096,256]{0,1:T(8,128)(2,1)}, u32[]{:S(2)}, u32[]{:S(2)}) %collective-permute-start.1) | collective-permute-done | bytes 2097184 | tf_op jit(solution)/shard_map/ppermute | solution.py:19
  351.1 3.2 constant_dynamic-update-slice_fusion.7
  354.3 3.1 constant_dynamic-update-slice_fusion.6
  357.4 1.5 constant_dynamic-update-slice_fusion.5
  359.0 32.4 %collective-permute-done.2 = bf16[4096,256]{0,1:T(8,128)(2,1)} collective-permute-done((bf16[4096,256]{0,1:T(8,128)(2,1)}, bf16[4096,256]{0,1:T(8,128)(2,1)}, u32[]{:S(2)}, u32[]{:S(2)}) %collective-permute-start.2) | collective-permute-done | bytes 2097184 | tf_op jit(solution)/shard_map/ppermute | solution.py:21
  391.4 3.2 constant_dynamic-update-slice_fusion.4
  394.5 3.1 constant_dynamic-update-slice_fusion.3
  397.7 1.4 convert_element_type.19
  399.1 0.9 copy-done.1
  399.9 0.8 slice.19
  400.8 3.2 constant_dynamic-update-slice_fusion.2
  404.0 1.6 constant_dynamic-update-slice_fusion.1
  405.6 3.1 constant_dynamic-update-slice_fusion
  408.7 12.3 %multiply_reduce_fusion = (f32[2]{0:T(128)S(1)}, f32[2,4096,896]{2,1,0:T(8,128)}) fusion(bf16[4096,2,64]{0,2,1:T(8,128)(2,1)S(1)} %bitcast.22, bf16[896,2,64]{0,2,1:T(8,128)(2,1)S(1)} %bitcast.23), kind=kOutput, calls=%fused_computation | convolution fusion | flops 954204160 | bytes 30638088 | tf_op jit(solution)/shard_map/isk,jsk->sij/dot_general | solution.py:53
  420.9 15.4 %all-gather.2.cloned.1.call-done = bf16[896,1024]{0,1:T(8,128)(2,1)} async-done(((bf16[896,256]{0,1:T(8,128)(2,1)}), bf16[896,1024]{0,1:T(8,128)(2,1)}) %all-gather.2.cloned.1.call-update) | async-done | bytes 1835024 | tf_op jit(solution)/shard_map/all_gather | solution.py:59
  436.3 3.5 convert_bitcast_fusion
  439.8 5.0 %copy.14 = f32[1024,896]{0,1:T(8,128)} copy(f32[1024,896]{1,0:T(8,128)} %convert_bitcast_fusion) | data formatting | bytes 7340032 | tf_op jit(solution)/shard_map/convert_element_type | solution.py:28
  444.8 24.0 %fusion.3 = f32[2,1024]{1,0:T(2,128)S(1)} fusion(f32[1024,896]{0,1:T(8,128)} %copy.14, bf16[4096,2048]{0,1:T(8,128)(2,1)} %constant_dynamic-update-slice_fusion, s32[]{:T(128)S(6)} %select_n.14, f32[2,4096,896]{2,1,0:T(8,128)} %get-tuple-element.5, f32[4096,896]{1,0:T(8,128)} %convert_add_fusion), kind=kOutput, calls=%fused_computation.8 | convolution fusion | flops 15050733568 | bytes 56107012 | tf_op jit(solution)/shard_map/it,nij->ntj/dot_general | solution.py:27
  468.9 0.1 reduce_sum.28
  469.0 16.2 %all-reduce = (f32[16,2]{0,1:T(2,128)S(1)}, f32[2]{0:T(128)S(1)}) all-reduce(f32[16,2]{0,1:T(2,128)S(1)} %bitcast.24, f32[2]{0:T(128)S(1)} %get-tuple-element.4), channel_id=1, replica_groups=mesh['dp'=4,'mp'=8] {'mp'}, use_global_device_ids=true, to_apply=%region_4.5 | all-reduce | flops 34 | bytes 272 | tf_op jit(solution)/shard_map/psum | solution.py:62
  485.2 0.6 broadcast_multiply_fusion
  485.8 0.5 broadcast_multiply_fusion.1
  (15 shorter events, 0.2 us)
Async XLA Ops:
  7.2 11.6 %copy-start.3 = (bf16[128,512]{1,0:T(8,128)(2,1)S(1)}, bf16[128,512]{1,0:T(8,128)(2,1)}, u32[]{:S(2)}) copy-start(bf16[128,512]{1,0:T(8,128)(2,1)} %param.7) | copy-start | bytes 393220
  7.2 11.6 %copy-start.2 = (bf16[256,512]{1,0:T(8,128)(2,1)S(1)}, bf16[256,512]{1,0:T(8,128)(2,1)}, u32[]{:S(2)}) copy-start(bf16[256,512]{1,0:T(8,128)(2,1)} %param.9) | copy-start | bytes 786436
  7.2 390.5 %reduce-scatter.2.cloned.1.call-start = ((), (), s32[]{:S(2)}) async-start(), calls=%async_computation.1 | async-start | bytes 12386304 | tf_op jit(solution)/shard_map/reduce_scatter | solution.py:43
  18.8 417.5 %all-gather.2.cloned.1.call-start = ((), (), s32[]{:S(2)}) async-start(), calls=%async_computation.2 | async-start | bytes 2293760 | tf_op jit(solution)/shard_map/all_gather | solution.py:59
  255.6 45.9 %collective-permute-start = (bf16[4096,256]{0,1:T(8,128)(2,1)}, bf16[4096,256]{0,1:T(8,128)(2,1)}, u32[]{:S(2)}, u32[]{:S(2)}) collective-permute-start(bf16[4096,256]{0,1:T(8,128)(2,1)} %slice.18), channel_id=1, source_target_pairs={{0,8},{8,16},{16,24},{24,0},{1,9},{9,17},{17,25},{25,1},{2,10},{10... | collective-permute-start | bytes 6291464 | tf_op jit(solution)/shard_map/ppermute | solution.py:19
  301.4 49.7 %collective-permute-start.1 = (bf16[4096,256]{0,1:T(8,128)(2,1)}, bf16[4096,256]{0,1:T(8,128)(2,1)}, u32[]{:S(2)}, u32[]{:S(2)}) collective-permute-start(bf16[4096,256]{0,1:T(8,128)(2,1)} %collective-permute-done), channel_id=1, source_target_pairs={{0,8},{8,16},{16,24},{24,0},{1,9},{9,17},{17,25},{25,1},{2,10},{10... | collective-permute-start | bytes 6291464 | tf_op jit(solution)/shard_map/ppermute | solution.py:19
  302.8 88.5 %collective-permute-start.2 = (bf16[4096,256]{0,1:T(8,128)(2,1)}, bf16[4096,256]{0,1:T(8,128)(2,1)}, u32[]{:S(2)}, u32[]{:S(2)}) collective-permute-start(bf16[4096,256]{0,1:T(8,128)(2,1)} %slice.18), channel_id=1, source_target_pairs={{0,24},{8,0},{16,8},{24,16},{1,25},{9,1},{17,9},{25,17},{2,26},{10... | collective-permute-start | bytes 6291464 | tf_op jit(solution)/shard_map/ppermute | solution.py:21
  399.1 0.9 copy-start.1
  400.7 7.9 %slice-start = ((bf16[896,384]{0,1:T(8,128)(2,1)}), bf16[896,128]{0,1:T(8,128)(2,1)S(1)}, s32[]{:S(2)}) async-start(bf16[896,384]{0,1:T(8,128)(2,1)} %copy-done.1), calls=%async_computation.3 | async-start | bytes 458752 | tf_op jit(solution)/shard_map/slice | solution.py:50
  400.8 7.9 %copy-start = (bf16[4096,128]{0,1:T(8,128)(2,1)S(1)}, bf16[4096,128]{0,1:T(8,128)(2,1)}, u32[]{:S(2)}) copy-start(bf16[4096,128]{0,1:T(8,128)(2,1)} %slice.16) | copy-start | bytes 3145732
Sparse Core Ops, SparseCore 0:
  18.9 212.7 reduce-scatter.1
  400.9 35.3 all-gather.1
